TPU v7x, 32 devices: a whole 2x2x4 slice. The times are simulated.
32 devices in a mesh: dp: 2 (over y), seq: 8 (over z, x), head: 2 (over core).
Axes of the slice: x: 2, y: 2, z: 4, core: 2. Of those that a mesh axis runs over, the one named last changes fastest.
Arguments:
- tokens: bfloat16 [2, 2, 1024, 2048], P(None, 'dp', 'seq'), may hold values from -6 to 6
- norm_gain: float32 [2048], replicated, may hold values from 0.5 to 1.5
- w_gate_in: bfloat16 [2048, 4096], P(('dp', 'seq'), 'head'), may hold values from -0.125 to 0.125
- w_x_in: bfloat16 [2048, 4096], P(('dp', 'seq'), 'head'), may hold values from -0.125 to 0.125
- w_bc_in: bfloat16 [2048, 256], P(('dp', 'seq')), may hold values from -0.125 to 0.125
- w_dt_in: bfloat16 [2048, 64], P(('dp', 'seq'), 'head'), may hold values from -0.0625 to 0.0625
- conv_x_w: float32 [4, 4096], P(None, 'head'), may hold values from -3 to 3
- conv_x_b: float32 [4096], P('head'), may hold values from -3 to 3
- conv_bc_w: float32 [4, 256], replicated, may hold values from -3 to 3
- conv_bc_b: float32 [256], replicated, may hold values from -3 to 3
- dt_bias: float32 [64], P('head'), may hold values from -7 to -2
- a_log: float32 [64], P('head'), may hold values from 0 to 1.5
- d_skip: float32 [64], P('head'), may hold values from 0.5 to 1.5
- gate_gain: float32 [4096], P('head'), may hold values from 0.5 to 1.5
- w_out: bfloat16 [4096, 2048], P('head', ('dp', 'seq')), may hold values from -0.09375 to 0.09375
- prefix_len: int32 [2, 2], P(None, 'dp'), may hold values from 102 to 1024, as said below
- cotangent: bfloat16 [2, 2, 1024, 2048], P(None, 'dp', 'seq'), may hold values from -6 to 6
Outputs:
- result: bfloat16 [2, 2, 1024, 2048], P(None, 'dp', 'seq')
- grad_tokens: float32 [2, 2, 1024, 2048], P(None, 'dp', 'seq')
- grad_norm_gain: float32 [2048], replicated
- grad_w_gate_in: float32 [2048, 4096], P(('dp', 'seq'), 'head')
- grad_w_x_in: float32 [2048, 4096], P(('dp', 'seq'), 'head')
- grad_w_bc_in: float32 [2048, 256], P(('dp', 'seq'))
- grad_w_dt_in: float32 [2048, 64], P(('dp', 'seq'), 'head')
- grad_conv_x_w: float32 [4, 4096], P(None, 'head')
- grad_conv_x_b: float32 [4096], P('head')
- grad_conv_bc_w: float32 [4, 256], replicated
- grad_conv_bc_b: float32 [256], replicated
- grad_dt_bias: float32 [64], P('head')
- grad_a_log: float32 [64], P('head')
- grad_d_skip: float32 [64], P('head')
- grad_gate_gain: float32 [4096], P('head')
- grad_w_out: float32 [4096, 2048], P('head', ('dp', 'seq'))
Inputs may be any that keep to these rules, and one draw needn't show every extreme that they name: Tokens before a sequence's prefix_len mix both ways; some sequence has exactly 1024 and some exactly 102.
All inputs are finite; a program needn't handle non-finite values.
Results may differ from a plain program's by a relative error of at most 0.012.
Values may be sent and summed in bfloat16 or wider, within the bound.
A program may use at most 256 MiB of HBM per device.

v0:
```python
import jax
import jax.numpy as jnp
from jax import lax
from jax.sharding import PartitionSpec as P

EPSILON = 1e-05
HIGHEST = lax.Precision.HIGHEST
BF16 = jnp.bfloat16
F32 = jnp.float32
CHUNK = 128


def dot_f32(a, b):
    return jnp.dot(a, b, preferred_element_type=F32)


def causal_conv(signal, kernel, bias):
    margin = kernel.shape[0] - 1
    length = signal.shape[1]
    padded = jnp.pad(signal, ((0, 0), (margin, 0), (0, 0)))
    summed = bias + jnp.zeros_like(signal)
    for offset in range(kernel.shape[0]):
        summed = summed + kernel[offset] * padded[:, offset : offset + length]
    return summed


def mixer(
    prefix, inner, bc, dt_raw, conv_x_w, conv_x_b, conv_bc_w, conv_bc_b, dt_bias, a_log, d_skip
):
    seqs, length, width = inner.shape
    heads = dt_raw.shape[-1]
    state = bc.shape[-1] // 2
    chunk = CHUNK
    count = length // chunk
    values = jax.nn.silu(causal_conv(inner, conv_x_w, conv_x_b))
    active = jax.nn.silu(causal_conv(bc, conv_bc_w, conv_bc_b))
    values = values.reshape(seqs, count, chunk, heads, width // heads)
    b_in = active[..., :state].reshape(seqs, count, chunk, state)
    c_out = active[..., state:].reshape(seqs, count, chunk, state)
    dt = jax.nn.softplus(dt_raw + dt_bias).reshape(seqs, count, chunk, heads)
    cum = jnp.cumsum(dt * -jnp.exp(a_log), axis=2)
    end = cum[:, :, -1:, :]
    places = jnp.arange(length, dtype=jnp.int32).reshape(count, chunk)
    inside = (places[None] < prefix[:, None, None])[..., None]
    weighted = values * dt[..., None]
    ends_state = jnp.einsum(
        "skth,skthp,sktn->skhpn", jnp.exp(end - cum), weighted, b_in, precision=HIGHEST
    )
    back_state = jnp.einsum(
        "skth,skthp,sktn->skhpn",
        jnp.where(inside, jnp.exp(cum), 0.0),
        weighted,
        b_in,
        precision=HIGHEST,
    )
    decay = jnp.exp(end[:, :, 0])[..., None, None]
    zero = jnp.zeros_like(ends_state[:, 0])
    state_in, back_in = ([zero], [zero])
    for k in range(count - 1):
        state_in.append(state_in[-1] * decay[:, k] + ends_state[:, k])
        back_in.append(back_in[-1] * decay[:, count - 1 - k] + back_state[:, count - 1 - k])
    state_in = jnp.stack(state_in, axis=1)
    back_in = jnp.stack(back_in[::-1], axis=1)
    scores = jnp.einsum("sktn,skun->sktu", c_out, b_in, precision=HIGHEST)
    spread = cum[:, :, :, None, :] - cum[:, :, None, :, :]
    behind = (places[:, :, None] >= places[:, None, :])[None, ..., None]
    ahead = (
        (places[:, :, None] < places[:, None, :])[None]
        & (places[None, :, None, :] < prefix[:, None, None, None])
    )[..., None]
    masked = jnp.where(behind, jnp.exp(jnp.where(behind, spread, 0.0)), 0.0) + jnp.where(
        ahead, jnp.exp(jnp.where(ahead, -spread, 0.0)), 0.0
    )
    out = jnp.einsum("sktuh,skuhp->skthp", scores[..., None] * masked, weighted, precision=HIGHEST)
    out = out + jnp.exp(cum)[..., None] * jnp.einsum(
        "sktn,skhpn->skthp", c_out, state_in, precision=HIGHEST
    )
    out = out + jnp.exp(end - cum)[..., None] * jnp.einsum(
        "sktn,skhpn->skthp", c_out, back_in, precision=HIGHEST
    )
    out = out + d_skip[:, None] * values
    return out.reshape(seqs, length, width)


def body(
    tokens,
    norm_gain,
    w_gate_in,
    w_x_in,
    w_bc_in,
    w_dt_in,
    conv_x_w,
    conv_x_b,
    conv_bc_w,
    conv_bc_b,
    dt_bias,
    a_log,
    d_skip,
    gate_gain,
    w_out,
    prefix_len,
    cotangent,
):
    dp, sq, hd = (lax.axis_size("dp"), lax.axis_size("seq"), lax.axis_size("head"))
    me_seq, me_head = (lax.axis_index("seq"), lax.axis_index("head"))
    micro, seqs, span, model = tokens.shape
    group = micro * seqs
    length = span * sq
    rows_here = group * span
    own_rows = rows_here // hd
    half = w_x_in.shape[1]
    width = half // sq
    heads = w_dt_in.shape[1] // sq
    full_inner = half * hd
    prefix = prefix_len.reshape(group)
    everyone = ("seq", "head")

    def mine(x):
        return lax.dynamic_slice_in_dim(
            x.reshape(rows_here, model), me_head * own_rows, own_rows, 0
        )

    def to_sequences(x):
        return x.reshape(sq, group, span, -1).transpose(1, 0, 2, 3).reshape(group, length, -1)

    def from_sequences(x):
        return x.reshape(group, sq, span, -1).transpose(1, 0, 2, 3).reshape(sq * rows_here, -1)

    def rms(x, gain):
        return x * lax.rsqrt(jnp.mean(x * x, axis=-1, keepdims=True) + EPSILON) * gain

    my_tokens = mine(tokens).astype(F32)
    my_cot = mine(cotangent)
    normed_own = rms(my_tokens, norm_gain).astype(BF16)
    normed = lax.all_gather(normed_own, everyone, axis=0, tiled=True)

    def columns(w):
        return lax.all_gather(
            lax.all_to_all(w, "seq", split_axis=1, concat_axis=0, tiled=True),
            "dp",
            axis=0,
            tiled=True,
        )

    wg = columns(w_gate_in)
    wx = columns(w_x_in)
    wd = lax.dynamic_slice_in_dim(
        lax.all_gather(w_dt_in, ("dp", "seq"), axis=0, tiled=True), me_seq * heads, heads, 1
    )
    wb = lax.all_gather(w_bc_in, ("dp", "seq"), axis=0, tiled=True)
    wo = lax.all_gather(
        lax.all_to_all(w_out, "seq", split_axis=0, concat_axis=1, tiled=True),
        "dp",
        axis=1,
        tiled=True,
    )
    cot = lax.all_gather(my_cot, everyone, axis=0, tiled=True)

    def part(x, size, axis):
        return lax.dynamic_slice_in_dim(x, me_seq * size, size, axis)

    cxw, cxb = (part(conv_x_w, width, 1), part(conv_x_b, width, 0))
    dtb, alog, dsk = (part(dt_bias, heads, 0), part(a_log, heads, 0), part(d_skip, heads, 0))
    gain = part(gate_gain, width, 0)

    def project(w):
        return to_sequences(dot_f32(normed, w).astype(BF16)).astype(F32)

    gate, inner, bc, dt_raw = (project(wg), project(wx), project(wb), project(wd))
    mixed, pull = jax.vjp(
        lambda *a: mixer(prefix, *a),
        inner,
        bc,
        dt_raw,
        cxw,
        cxb,
        conv_bc_w,
        conv_bc_b,
        dtb,
        alog,
        dsk,
    )
    sig = jax.nn.sigmoid(gate)
    act = gate * sig
    gated = mixed * act
    grad_scaled = to_sequences(jnp.einsum("rd,kd->rk", cot, wo, preferred_element_type=F32))
    gs = grad_scaled * gain
    sums = lax.psum(
        jnp.stack([jnp.sum(gated * gated, axis=-1), jnp.sum(gs * gated, axis=-1)]), everyone
    )
    scale = lax.rsqrt(sums[0][..., None] / full_inner + EPSILON)
    unit = gated * scale
    scaled = from_sequences((unit * gain).astype(BF16))
    branch = lax.psum_scatter(
        dot_f32(scaled, wo).astype(BF16), everyone, scatter_dimension=0, tiled=True
    )
    result_own = (my_tokens + branch.astype(F32)).astype(BF16)
    grad_gain = jnp.sum(grad_scaled * unit, axis=(0, 1))
    grad_wo = jnp.einsum("rk,rd->kd", scaled, cot, preferred_element_type=F32)
    grad_gated = gs * scale - gated * (scale * scale * scale * (sums[1][..., None] / full_inner))
    grad_mixed = grad_gated * act
    grad_gate = grad_gated * mixed * (sig * (1.0 + gate * (1.0 - sig)))
    d_inner, d_bc, d_dt, d_cxw, d_cxb, d_cbw, d_cbb, d_dtb, d_alog, d_dsk = pull(grad_mixed)
    gg = from_sequences(grad_gate.astype(BF16))
    gx = from_sequences(d_inner.astype(BF16))
    gd = from_sequences(d_dt.astype(BF16))
    gb_own = lax.psum_scatter(
        from_sequences(d_bc), everyone, scatter_dimension=0, tiled=True
    ).astype(BF16)

    def inward(g, w):
        return jnp.einsum("rc,kc->rk", g, w, preferred_element_type=F32)

    def weight_grad(n, g):
        return jnp.einsum("rk,rc->kc", n, g, preferred_element_type=F32)

    part_normed = inward(gg, wg) + inward(gx, wx) + inward(gd, wd)
    grad_normed = lax.psum_scatter(
        part_normed.astype(BF16), everyone, scatter_dimension=0, tiled=True
    ).astype(F32) + inward(gb_own, wb)
    _, pull_norm = jax.vjp(rms, my_tokens, norm_gain)
    grad_rows, grad_norm = pull_norm(grad_normed)
    grad_own = my_cot.astype(F32) + grad_rows

    def home(g):
        return lax.all_to_all(
            lax.psum_scatter(g.astype(BF16), "dp", scatter_dimension=0, tiled=True),
            "seq",
            split_axis=0,
            concat_axis=1,
            tiled=True,
        ).astype(F32)

    g_gate, g_x = (home(weight_grad(normed, gg)), home(weight_grad(normed, gx)))
    g_dt = lax.all_to_all(
        lax.psum_scatter(weight_grad(normed, gd), "dp", scatter_dimension=0, tiled=True),
        "seq",
        split_axis=0,
        concat_axis=1,
        tiled=True,
    )
    g_bc = lax.psum_scatter(
        lax.psum(weight_grad(normed_own, gb_own), "head"),
        ("dp", "seq"),
        scatter_dimension=0,
        tiled=True,
    )
    g_out = lax.all_to_all(
        lax.psum_scatter(grad_wo.astype(BF16), "dp", scatter_dimension=1, tiled=True),
        "seq",
        split_axis=1,
        concat_axis=0,
        tiled=True,
    ).astype(F32)

    def whole(x):
        return lax.all_gather(x, "head", axis=0, tiled=True).reshape(micro, seqs, span, model)

    small = lax.psum((d_cxw, d_cxb, d_dtb, d_alog, d_dsk, grad_gain), "dp")
    small = [lax.all_gather(a, "seq", axis=a.ndim - 1, tiled=True) for a in small]
    grad_norm, d_cbw, d_cbb = lax.psum((grad_norm, d_cbw, d_cbb), ("dp", "seq", "head"))
    return (
        whole(result_own),
        whole(grad_own),
        grad_norm,
        g_gate,
        g_x,
        g_bc,
        g_dt,
        small[0],
        small[1],
        d_cbw,
        d_cbb,
        small[2],
        small[3],
        small[4],
        small[5],
        g_out,
    )


def solution(mesh):
    rows = P(("dp", "seq"), "head")
    tok = P(None, "dp", "seq", None)
    return jax.shard_map(
        body,
        mesh=mesh,
        in_specs=(
            tok,
            P(),
            rows,
            rows,
            P(("dp", "seq"), None),
            rows,
            P(None, "head"),
            P("head"),
            P(),
            P(),
            P("head"),
            P("head"),
            P("head"),
            P("head"),
            P("head", ("dp", "seq")),
            P(None, "dp"),
            tok,
        ),
        out_specs=(
            tok,
            tok,
            P(),
            rows,
            rows,
            P(("dp", "seq"), None),
            rows,
            P(None, "head"),
            P("head"),
            P(),
            P(),
            P("head"),
            P("head"),
            P("head"),
            P("head"),
            P("head", ("dp", "seq")),
        ),
        check_vma=False,
    )
```

profile of v0, /device:TPU:14, one launch (start us, length us, event | category | flops | bytes accessed | tf_op | source)
XLA Modules:
  0.0 1105.0 jit_solution(2029383470495228353)
XLA Ops:
  12.0 27.5 %all_to_all.115 = bf16[128,8,256]{0,2,1:T(8,128)(2,1)S(1)} all-to-all(bf16[128,8,256]{0,2,1:T(8,128)(2,1)S(1)} %bitcast.572), channel_id=1, replica_groups=mesh['dp'=2,'seq'=8,'head'=2] {'seq'}, dimensions={1} | all-to-all | bytes 1048576 | tf_op jit(solution)/shard_map/all_to_all | solution.py:139
  41.4 28.8 %all_to_all.116 = bf16[8,256,128]{2,1,0:T(8,128)(2,1)S(1)} all-to-all(bf16[8,256,128]{2,1,0:T(8,128)(2,1)S(1)} %bitcast.582), channel_id=1, replica_groups=mesh['dp'=2,'seq'=8,'head'=2] {'seq'}, dimensions={0} | all-to-all | bytes 1048576 | tf_op jit(solution)/shard_map/all_to_all | solution.py:152
  73.2 8.3 all-to-all-start.1
  83.4 42.2 %all_gather.47 = bf16[2048,32]{0,1:T(8,128)(2,1)S(1)} all-gather(bf16[128,32]{0,1:T(8,128)(2,1)S(1)} %copy-done.97), channel_id=1, replica_groups=mesh['dp'=2,'seq'=8,'head'=2] {'dp','seq'}, dimensions={0}, use_global_device_ids=true | all-gather | bytes 139264 | tf_op jit(solution)/shard_map/all_gather | solution.py:148
  129.6 5.6 fusion.19
  135.8 47.9 %fusion.184 = f32[2,8,128,4]{3,1,2,0:T(8,128)S(1)} fusion(f32[2,8,128,4]{3,1,2,0:T(8,128)S(1)} %copy.524), kind=kOutput, calls=%fused_computation.362 | output fusion | flops 1040384 | bytes 65536 | tf_op jit(solution)/shard_map/jvp(jit(cumsum))/reduce_window_sum | solution.py:41
  184.5 6.0 convolution_convert_fusion.6
  192.2 6.0 convolution_convert_fusion.5
  198.6 12.3 %all-gather.21.cloned.1.call-done = bf16[256,2048]{0,1:T(8,128)(2,1)} async-done(((bf16[256,1024]{0,1:T(8,128)(2,1)}), bf16[256,2048]{0,1:T(8,128)(2,1)}) %all-gather.21.cloned.1.call-update) | async-done | bytes 1048592 | tf_op jit(solution)/shard_map/all_gather | solution.py:151
  210.9 76.9 %all-gather.19.cloned.1.call-done = bf16[2048,2048]{1,0:T(8,128)(2,1)} async-done(((bf16[128,2048]{1,0:T(8,128)(2,1)}), bf16[2048,2048]{1,0:T(8,128)(2,1)}) %all-gather.19.cloned.1.call-update) | async-done | bytes 8388624 | tf_op jit(solution)/shard_map/all_gather | solution.py:157
  287.8 7.3 fusion.188
  298.3 11.7 %all-gather.17.cloned.1.call-done = bf16[2048,256]{1,0:T(8,128)(2,1)} async-done(((bf16[1024,256]{1,0:T(8,128)(2,1)}), bf16[2048,256]{1,0:T(8,128)(2,1)}) %all-gather.17.cloned.1.call-update) | async-done | bytes 1048592 | tf_op jit(solution)/shard_map/all_gather | solution.py:138
  310.0 6.0 convolution_convert_fusion.4
  321.4 6.9 fusion.44
  328.3 5.1 reshape.593
  333.3 4.9 copy.522
  356.7 10.7 multiply_reduce_fusion.16
  373.1 48.8 %psum.77 = f32[2,2,1024]{2,1,0:T(2,128)S(1)} all-reduce(f32[2,2,1024]{2,1,0:T(2,128)S(1)} %pad_maximum_fusion), channel_id=1, replica_groups=mesh['dp'=2,'seq'=8,'head'=2] {'seq','head'}, use_global_device_ids=true, to_apply=%region_4.5 | all-reduce | flops 4096 | bytes 32768 | tf_op jit(solution)/shard_map/psum | solution.py:188
  423.2 5.9 multiply_reduce_fusion.13
  455.2 12.5 %fusion.12 = (f32[2,8,128,128]{3,2,1,0:T(8,128)}, f32[2,8,128,128,4]{3,2,4,1,0:T(8,128)}) fusion(f32[2,8,128,4]{2,3,1,0:T(4,128)S(1)} %copy-done.72, pred[2,8,128,128]{3,2,1,0:T(8,128)(4,1)S(1)} %copy-done.51, pred[8,128,128]{2,1,0:T(8,128)(4,1)S(1)} %copy-done.56, f32[2,8,128,128]{3,2,1,0:T(8,128)S(1)} %copy-done.41, ...), kind=kOutput, calls=%fused_computation.18 | convolution fusion | flops 824442880 | bytes 10944512 | tf_op jit(solution)/shard_map/transpose(jvp(sktuh,skuhp->skthp))/dot_general | solution.py:74
  478.7 9.8 multiply_reduce_fusion
  491.9 47.3 %fusion.185 = f32[2,8,128,4]{3,1,2,0:T(8,128)S(1)} fusion(f32[2,8,128,4]{3,1,2,0:T(8,128)S(1)} %copy.609), kind=kOutput, calls=%fused_computation.363 | output fusion | flops 1040384 | bytes 65536 | tf_op jit(solution)/shard_map/transpose(jvp(jit(cumsum)))/reduce_window_sum | solution.py:41
  539.8 4.8 copy.658
  544.6 5.8 reshape.594
  566.2 8.1 fusion.156
  577.5 8.4 fusion.189
  585.9 16.1 %add_convert_fusion = bf16[2048,2048]{1,0:T(8,128)(2,1)} fusion(f32[2048,2048]{1,0:T(8,128)} %fusion.156, f32[2048,2048]{1,0:T(8,128)} %fusion.189, bf16[2048,256]{1,0:T(8,128)(2,1)S(1)} %bitcast.562, bf16[2048,256]{1,0:T(8,128)(2,1)S(1)} %copy-done.36), kind=kOutput, calls=%fused_computation | convolution fusion | flops 2160066560 | bytes 44040192 | tf_op jit(solution)/shard_map/rc,kc->rk/dot_general | solution.py:212
  603.5 5.6 convolution_convert_fusion
  609.2 6.9 fusion.190
  616.4 6.9 convolution_convert_fusion.3
  623.4 7.0 convolution_convert_fusion.2
  630.4 6.9 convolution_convert_fusion.1
  640.3 105.5 %reduce-scatter.13.cloned.1.call-done = bf16[128,2048]{1,0:T(8,128)(2,1)} async-done(((bf16[2048,2048]{1,0:T(8,128)(2,1)}), bf16[128,2048]{1,0:T(8,128)(2,1)}) %reduce-scatter.13.cloned.1.call-update) | async-done | bytes 524304 | tf_op jit(solution)/shard_map/reduce_scatter | solution.py:218
  747.9 106.9 %reduce-scatter.11.cloned.1.call-done = bf16[128,2048]{1,0:T(8,128)(2,1)} async-done(((bf16[2048,2048]{1,0:T(8,128)(2,1)}), bf16[128,2048]{1,0:T(8,128)(2,1)}) %reduce-scatter.11.cloned.1.call-update) | async-done | bytes 524304 | tf_op jit(solution)/shard_map/reduce_scatter | solution.py:194
  857.4 19.1 %reduce-scatter.25.cloned.1.call-done = f32[1024,4]{1,0:T(8,128)} async-done(((f32[2048,4]{1,0:T(8,128)}), f32[1024,4]{1,0:T(8,128)}) %reduce-scatter.25.cloned.1.call-update) | async-done | bytes 16400
  877.7 10.1 all_to_all.117
  887.8 11.9 %reduce-scatter.17.cloned.1.call-done = bf16[1024,256]{1,0:T(8,128)(2,1)} async-done(((bf16[2048,256]{1,0:T(8,128)(2,1)}), bf16[1024,256]{1,0:T(8,128)(2,1)}) %reduce-scatter.17.cloned.1.call-update) | async-done | bytes 524304 | tf_op jit(solution)/shard_map/reduce_scatter | solution.py:227
  899.7 6.0 all-to-all-start.3
  906.3 16.5 %reduce-scatter.19.cloned.1.call-done = bf16[1024,256]{1,0:T(8,128)(2,1)} async-done(((bf16[2048,256]{1,0:T(8,128)(2,1)}), bf16[1024,256]{1,0:T(8,128)(2,1)}) %reduce-scatter.19.cloned.1.call-update) | async-done | bytes 524304 | tf_op jit(solution)/shard_map/reduce_scatter | solution.py:227
  922.8 6.0 all-to-all-start.4
  930.3 15.1 %reduce-scatter.21.cloned.1.call-done = bf16[256,1024]{1,0:T(8,128)(2,1)} async-done(((bf16[256,2048]{1,0:T(8,128)(2,1)}), bf16[256,1024]{1,0:T(8,128)(2,1)}) %reduce-scatter.21.cloned.1.call-update) | async-done | bytes 524304 | tf_op jit(solution)/shard_map/reduce_scatter | solution.py:249
  947.3 6.0 all-to-all-start.6
  953.5 5.0 all-reduce.54
  958.5 19.4 %all-gather = f32[8,1,256]{2,1,0:T(1,128)S(1)} all-gather(f32[1,1,256]{2,1,0:T(1,128)S(1)} %bitcast.633), channel_id=1, replica_groups=mesh['dp'=2,'seq'=8,'head'=2] {'seq'}, dimensions={0}, use_global_device_ids=true | all-gather | bytes 9216 | tf_op jit(solution)/shard_map/all_gather | solution.py:260
  977.9 15.5 %all-gather.1 = f32[8,1,256]{2,1,0:T(1,128)S(1)} all-gather(f32[1,1,256]{2,1,0:T(1,128)S(1)} %bitcast.632), channel_id=1, replica_groups=mesh['dp'=2,'seq'=8,'head'=2] {'seq'}, dimensions={0}, use_global_device_ids=true | all-gather | bytes 9216 | tf_op jit(solution)/shard_map/all_gather | solution.py:260
  993.4 27.9 %all_gather.54 = f32[4,2048]{1,0:T(4,128)S(1)} all-gather(f32[4,256]{1,0:T(4,128)S(1)} %get-tuple-element.164), channel_id=1, replica_groups=mesh['dp'=2,'seq'=8,'head'=2] {'seq'}, dimensions={1}, use_global_device_ids=true | all-gather | bytes 36864 | tf_op jit(solution)/shard_map/all_gather | solution.py:260
  1021.9 22.0 %all-reduce.53 = (f32[32]{0:T(128)}, f32[32]{0:T(128)}, f32[32]{0:T(128)}) all-reduce(f32[32]{0:T(128)S(1)} %dynamic-update-slice, f32[32]{0:T(128)S(1)} %dynamic-update-slice.1, f32[32]{0:T(128)S(1)} %dynamic-update-slice.2), channel_id=1, replica_groups=mesh['dp'=2,'seq'=8,'head'=2] {'seq'}, use_global_device_ids=true, to_apply=%add.49 | all-reduce | flops 96 | bytes 768
  1047.4 43.9 %all-reduce.52 = (f32[2048]{0:T(1024)}, f32[4,256]{1,0:T(4,128)}, f32[256]{0:T(256)}) all-reduce(f32[2048]{0:T(1024)S(1)} %get-tuple-element.135, f32[4,256]{1,0:T(4,128)S(1)} %pad_add_fusion.10, f32[256]{0:T(256)S(1)} %get-tuple-element.131), channel_id=1, replica_groups=mesh['dp'=2,'seq'=8,'head'=2] {'dp','seq','head'}, use_global_device_ids=true, to_apply=%region_33.34 | all-reduce | flops 3328 | bytes 26624 | tf_op jit(solution)/shard_map/psum | solution.py:261
  (421 shorter events, 136.7 us)
Async XLA Ops:
  7.2 122.4 %all-gather.11.cloned.1.call-start = ((), (), s32[]{:S(2)}) async-start(), calls=%async_computation.15 | async-start | bytes 8912896 | tf_op jit(solution)/shard_map/all_gather | solution.py:135
  11.7 172.8 %all-gather.13.cloned.1.call-start = ((), (), s32[]{:S(2)}) async-start(), calls=%async_computation.16 | async-start | bytes 1572864 | tf_op jit(solution)/shard_map/all_gather | solution.py:138
  40.6 151.7 %all-gather.15.cloned.1.call-start = ((), (), s32[]{:S(2)}) async-start(), calls=%async_computation.17 | async-start | bytes 1114112 | tf_op jit(solution)/shard_map/all_gather | solution.py:150
  41.3 169.6 %all-gather.21.cloned.1.call-start = ((), (), s32[]{:S(2)}) async-start(), calls=%async_computation.20 | async-start | bytes 1572864 | tf_op jit(solution)/shard_map/all_gather | solution.py:151
  71.3 54.3 %copy-start.112 = (f32[32]{0:T(128)S(1)}, f32[32]{0:T(128)}, u32[]{:S(2)}) copy-start(f32[32]{0:T(128)} %param.27) | copy-start | bytes 388
  71.3 54.4 %copy-start.113 = (f32[32]{0:T(128)S(1)}, f32[32]{0:T(128)}, u32[]{:S(2)}) copy-start(f32[32]{0:T(128)} %param.29) | copy-start | bytes 388
  71.3 56.6 %copy-start.108 = (s32[2,1]{0,1:T(1,128)S(1)}, s32[2,1]{0,1:T(1,128)}, u32[]{:S(2)}) copy-start(s32[2,1]{0,1:T(1,128)} %param.32) | copy-start | bytes 28
  71.3 56.7 %copy-start.104 = (f32[4,256]{1,0:T(4,128)S(1)}, f32[4,256]{1,0:T(4,128)}, u32[]{:S(2)}) copy-start(f32[4,256]{1,0:T(4,128)} %param.25) | copy-start | bytes 12292
  71.3 216.5 %all-gather.19.cloned.1.call-start = ((), (), s32[]{:S(2)}) async-start(), calls=%async_computation.19 | async-start | bytes 8912896 | tf_op jit(solution)/shard_map/all_gather | solution.py:157
  73.2 55.2 %all-to-all-start.1 = ((bf16[128,8,256]{0,2,1:T(8,128)(2,1)}), bf16[128,8,256]{0,2,1:T(8,128)(2,1)S(1)}, u32[]{:S(2)}, u32[]{:S(2)}) async-start(bf16[128,8,256]{0,2,1:T(8,128)(2,1)} %bitcast.42), calls=%async_computation.1 | async-start | bytes 1048576 | tf_op jit(solution)/shard_map/all_to_all | solution.py:139
  81.6 228.4 %all-gather.17.cloned.1.call-start = ((), (), s32[]{:S(2)}) async-start(), calls=%async_computation.18 | async-start | bytes 1572864 | tf_op jit(solution)/shard_map/all_gather | solution.py:138
  81.7 53.6 %copy-start.100 = (f32[4]{0:T(128)}, f32[4]{0:T(128)S(1)}, u32[]{:S(2)}) copy-start(f32[4]{0:T(128)S(1)} %fusion.174) | copy-start | bytes 52
  82.6 238.7 %copy-start.81 = (f32[1,256]{1,0:T(1,128)}, f32[1,256]{1,0:T(1,128)S(1)}, u32[]{:S(2)}) copy-start(f32[1,256]{1,0:T(1,128)S(1)} %get-tuple-element.230) | copy-start | bytes 3076
  82.6 238.7 %copy-start.83 = (f32[1,256]{1,0:T(1,128)}, f32[1,256]{1,0:T(1,128)S(1)}, u32[]{:S(2)}) copy-start(f32[1,256]{1,0:T(1,128)S(1)} %get-tuple-element.231) | copy-start | bytes 3076
  82.6 238.7 %copy-start.85 = (f32[1,256]{1,0:T(1,128)}, f32[1,256]{1,0:T(1,128)S(1)}, u32[]{:S(2)}) copy-start(f32[1,256]{1,0:T(1,128)S(1)} %get-tuple-element.232) | copy-start | bytes 3076
  82.6 238.7 %copy-start.87 = (f32[1,256]{1,0:T(1,128)}, f32[1,256]{1,0:T(1,128)S(1)}, u32[]{:S(2)}) copy-start(f32[1,256]{1,0:T(1,128)S(1)} %get-tuple-element.233) | copy-start | bytes 3076
  125.7 230.9 %copy-start.115 = (f32[4]{0:T(128)}, f32[4]{0:T(128)S(1)}, u32[]{:S(2)}) copy-start(f32[4]{0:T(128)S(1)} %dynamic_slice.33) | copy-start | bytes 52
  128.0 70.2 %copy-start.67 = (pred[2,8,128]{2,1,0:T(8,128)(4,1)}, pred[2,8,128]{2,1,0:T(8,128)(4,1)S(1)}, u32[]{:S(2)}) copy-start(pred[2,8,128]{2,1,0:T(8,128)(4,1)S(1)} %broadcast_compare_fusion.2) | copy-start | bytes 6148
  128.0 210.3 %copy-start.89 = (f32[1,256]{1,0:T(1,128)}, f32[1,256]{1,0:T(1,128)S(1)}, u32[]{:S(2)}) copy-start(f32[1,256]{1,0:T(1,128)S(1)} %get-tuple-element.239) | copy-start | bytes 3076
  128.0 210.3 %copy-start.91 = (f32[1,256]{1,0:T(1,128)}, f32[1,256]{1,0:T(1,128)S(1)}, u32[]{:S(2)}) copy-start(f32[1,256]{1,0:T(1,128)S(1)} %get-tuple-element.240) | copy-start | bytes 3076
  128.0 210.3 %copy-start.93 = (f32[1,256]{1,0:T(1,128)}, f32[1,256]{1,0:T(1,128)S(1)}, u32[]{:S(2)}) copy-start(f32[1,256]{1,0:T(1,128)S(1)} %get-tuple-element.241) | copy-start | bytes 3076
  128.0 210.3 %copy-start.95 = (f32[1,256]{1,0:T(1,128)}, f32[1,256]{1,0:T(1,128)S(1)}, u32[]{:S(2)}) copy-start(f32[1,256]{1,0:T(1,128)S(1)} %get-tuple-element.242) | copy-start | bytes 3076
  128.3 228.4 %copy-start.55 = (pred[8,128,128]{2,1,0:T(8,128)(4,1)}, pred[8,128,128]{2,1,0:T(8,128)(4,1)S(1)}, u32[]{:S(2)}) copy-start(pred[8,128,128]{2,1,0:T(8,128)(4,1)S(1)} %get-tuple-element.237) | copy-start | bytes 393220
  128.4 228.2 %copy-start.50 = (pred[2,8,128,128]{3,2,1,0:T(8,128)(4,1)}, pred[2,8,128,128]{3,2,1,0:T(8,128)(4,1)S(1)}, u32[]{:S(2)}) copy-start(pred[2,8,128,128]{3,2,1,0:T(8,128)(4,1)S(1)} %broadcast_and_fusion) | copy-start | bytes 786436
  129.5 508.0 %reduce-scatter.15.cloned.1.call-start = ((), (), s32[]{:S(2)}) async-start(), calls=%async_computation.24 | async-start | bytes 2228224 | tf_op jit(solution)/shard_map/reduce_scatter | solution.py:207
  184.5 172.2 %copy-start.71 = (f32[2,8,128,4]{2,3,1,0:T(4,128)}, f32[2,8,128,4]{2,3,1,0:T(4,128)S(1)}, u32[]{:S(2)}) copy-start(f32[2,8,128,4]{2,3,1,0:T(4,128)S(1)} %copy.525) | copy-start | bytes 98308
  198.4 148.2 %copy-start.59 = (f32[2,8,128,4]{2,3,1,0:T(4,128)}, f32[2,8,128,4]{2,3,1,0:T(4,128)S(1)}, u32[]{:S(2)}) copy-start(f32[2,8,128,4]{2,3,1,0:T(4,128)S(1)} %copy.546) | copy-start | bytes 98308
  198.6 139.7 %copy-start = (f32[8,2,128,256]{3,2,0,1:T(8,128)}, f32[8,2,128,256]{3,2,0,1:T(8,128)S(1)}, u32[]{:S(2)}) copy-start(f32[8,2,128,256]{3,2,0,1:T(8,128)S(1)} %copy.523) | copy-start | bytes 6291460
  566.1 179.7 %reduce-scatter.13.cloned.1.call-start = ((), (), s32[]{:S(2)}) async-start(), calls=%async_computation.23 | async-start | bytes 8912896 | tf_op jit(solution)/shard_map/reduce_scatter | solution.py:218
  602.0 252.8 %reduce-scatter.11.cloned.1.call-start = ((), (), s32[]{:S(2)}) async-start(), calls=%async_computation.21 | async-start | bytes 8912896 | tf_op jit(solution)/shard_map/reduce_scatter | solution.py:194
  609.1 267.4 %reduce-scatter.25.cloned.1.call-start = ((), (), s32[]{:S(2)}) async-start(), calls=%async_computation.31 | async-start | bytes 1572864
  616.1 283.6 %reduce-scatter.17.cloned.1.call-start = ((), (), s32[]{:S(2)}) async-start(), calls=%async_computation.26 | async-start | bytes 1572864 | tf_op jit(solution)/shard_map/reduce_scatter | solution.py:227
  623.3 299.5 %reduce-scatter.19.cloned.1.call-start = ((), (), s32[]{:S(2)}) async-start(), calls=%async_computation.27 | async-start | bytes 1572864 | tf_op jit(solution)/shard_map/reduce_scatter | solution.py:227
  630.4 315.0 %reduce-scatter.21.cloned.1.call-start = ((), (), s32[]{:S(2)}) async-start(), calls=%async_computation.28 | async-start | bytes 1572864 | tf_op jit(solution)/shard_map/reduce_scatter | solution.py:249
  637.3 108.5 %copy-start.31 = (bf16[2,1,128,2048]{3,2,1,0:T(8,128)(2,1)S(1)}, bf16[2,1,128,2048]{3,2,1,0:T(8,128)(2,1)}, u32[]{:S(2)}) copy-start(bf16[2,1,128,2048]{3,2,1,0:T(8,128)(2,1)} %param.17) | copy-start | bytes 3145732
  637.3 108.5 %copy-start.62 = (f32[2048]{0:T(1024)S(1)}, f32[2048]{0:T(1024)}, u32[]{:S(2)}) copy-start(f32[2048]{0:T(1024)} %param.18) | copy-start | bytes 24580
  637.4 108.5 %copy-start.99 = (f32[128]{0:T(128)S(1)}, f32[128]{0:T(128)}, u32[]{:S(2)}) copy-start(f32[128]{0:T(128)} %copy-done.98) | copy-start | bytes 1540
  637.4 406.7 %reduce-scatter.23.cloned.1.call-start = ((), (), s32[]{:S(2)}) async-start(), calls=%async_computation.29 | async-start | bytes 2228224 | tf_op jit(solution)/shard_map/reduce_scatter | solution.py:242
  637.5 108.4 %copy-start.49 = (f32[128,256]{1,0:T(8,128)S(1)}, f32[128,256]{1,0:T(8,128)}, u32[]{:S(2)}) copy-start(f32[128,256]{1,0:T(8,128)} %reduce-scatter.15.cloned.1.call-done) | copy-start | bytes 393220
  640.3 107.6 %copy-start.111 = (f32[128]{0:T(128)S(1)}, f32[128]{0:T(128)}, u32[]{:S(2)}) copy-start(f32[128]{0:T(128)} %copy-done.110) | copy-start | bytes 1540
  640.3 214.5 %copy-start.44 = (bf16[2,1,128,2048]{3,2,1,0:T(8,128)(2,1)S(1)}, bf16[2,1,128,2048]{3,2,1,0:T(8,128)(2,1)}, u32[]{:S(2)}) copy-start(bf16[2,1,128,2048]{3,2,1,0:T(8,128)(2,1)} %param.33) | copy-start | bytes 3145732
  640.3 451.1 %all-gather.23.cloned.1.call-start = ((), (), s32[]{:S(2)}) async-start(), calls=%async_computation.22 | async-start | bytes 1572864 | tf_op jit(solution)/shard_map/all_gather | solution.py:257
  857.4 71.5 %copy-start.114 = (u32[32]{0:T(128)S(1)}, u32[32]{0:T(128)}, u32[]{:S(2)}) copy-start(u32[32]{0:T(128)} %constant.176) | copy-start | bytes 388
  899.7 23.1 %all-to-all-start.3 = ((bf16[8,128,256]{2,1,0:T(8,128)(2,1)}), bf16[8,128,256]{2,1,0:T(8,128)(2,1)S(1)}, u32[]{:S(2)}, u32[]{:S(2)}) async-start(bf16[8,128,256]{2,1,0:T(8,128)(2,1)} %bitcast.584), calls=%async_computation.7 | async-start | bytes 1048576 | tf_op jit(solution)/shard_map/all_to_all | solution.py:226
  905.7 185.6 %all-gather.25.cloned.1.call-start = ((), (), s32[]{:S(2)}) async-start(), calls=%async_computation.25 | async-start | bytes 3145728 | tf_op jit(solution)/shard_map/all_gather | solution.py:257
  922.8 24.5 %all-to-all-start.4 = ((bf16[8,128,256]{2,1,0:T(8,128)(2,1)}), bf16[8,128,256]{2,1,0:T(8,128)(2,1)S(1)}, u32[]{:S(2)}, u32[]{:S(2)}) async-start(bf16[8,128,256]{2,1,0:T(8,128)(2,1)} %bitcast.583), calls=%async_computation.9 | async-start | bytes 1048576 | tf_op jit(solution)/shard_map/all_to_all | solution.py:226
  947.3 99.0 %all-to-all-start.6 = ((bf16[256,8,128]{2,0,1:T(8,128)(2,1)}), bf16[256,8,128]{2,0,1:T(8,128)(2,1)S(1)}, u32[]{:S(2)}, u32[]{:S(2)}) async-start(bf16[256,8,128]{2,0,1:T(8,128)(2,1)} %copy_bitcast_fusion), calls=%async_computation.12 | async-start | bytes 1048576 | tf_op jit(solution)/shard_map/all_to_all | solution.py:248
  953.4 138.0 %all-reduce.57.cloned.1.call-start = ((), (), s32[]{:S(2)}) async-start(), calls=%async_computation.30 | async-start | bytes 262144 | tf_op jit(solution)/shard_map/psum | solution.py:243
  (90 other events, 876.7 us)
Sparse Core Ops, SparseCore 0:
  11.8 92.2 all-gather.10
  106.2 24.0 all-gather.12
  133.1 54.8 all-gather.14
  190.0 20.8 all-gather.20
  213.5 74.2 all-gather.18
  289.8 20.1 all-gather.16
  566.2 70.9 reduce-scatter.14
  641.8 103.9 reduce-scatter.12
  750.4 104.3 reduce-scatter.10
  857.6 18.9 reduce-scatter.24
  879.3 20.3 reduce-scatter.16
  902.5 20.3 reduce-scatter.18
  925.1 20.3 reduce-scatter.20
  948.2 76.7 reduce-scatter.22
  1026.4 14.1 all-gather.22
  1042.7 11.7 all-gather.24
  1056.8 19.0 all-reduce.56
where the time goes:
time: 1110 us; the launch traced here: 1100 us
  waiting for transfers between devices  377 us (34%)
  blocking collectives  291 us (26%)
  matrix products  176 us (16%)
  other arithmetic  145 us (13%)
  local copies, waits for them, and re-layouts  72 us (6%)
  starting transfers between devices  27.2 us (2%)
  between operations  16.4 us (1%)
    reduce_scatter x1, waiting for transfers between devices, body(): lax.psum_scatter(dot_f32(scaled, wo).astype(BF16), everyone, scatter_dime...  107 us
    reduce_scatter x1, waiting for transfers between devices, body(): lax.psum_scatter(part_normed.astype(BF16), everyone, scatter_dimension=0,...  105 us
    another operation x2, other arithmetic, mixer(): cum = jnp.cumsum(dt * -jnp.exp(a_log), axis=2)  95.2 us
    all_gather x1, waiting for transfers between devices, body(): cot = lax.all_gather(my_cot, everyone, axis=0, tiled=True)  76.9 us
    all_gather x3, blocking collectives, body(): lax.all_gather(a, 'seq', axis=a.ndim - 1, tiled=True)  62.8 us
    psum x1, blocking collectives, body(): lax.psum(jnp.stack([jnp.sum(gated * gated, axis=-1), jnp.sum(gs * gated,...  48.8 us
    psum x1, blocking collectives, body(): lax.psum((grad_norm, d_cbw, d_cbb), ('dp', 'seq', 'head'))  43.9 us
    all_gather x1, blocking collectives, body(): lax.all_gather(w_dt_in, ('dp', 'seq'), axis=0, tiled=True)  42.2 us
  transfers between devices with their start and end apart: 21, of which 9 were waited for; matrix products, arithmetic and copies ran while one was open for 16% of the time, Pallas kernels for 0%

commit v1 on v0

--- a/solution.py
+++ b/solution.py
@@ -149,7 +149,10 @@
     )
     wb = lax.all_gather(w_bc_in, ("dp", "seq"), axis=0, tiled=True)
     wo = lax.all_gather(
-        lax.all_to_all(w_out, "seq", split_axis=0, concat_axis=1, tiled=True),
+        jnp.concatenate(
+            lax.all_to_all(jnp.stack(jnp.split(w_out, lax.axis_size("seq"), axis=0)), "seq", 0, 0),
+            axis=1,
+        ),
         "dp",
         axis=1,
         tiled=True,

time: 1110 us -> 1110 us (level)
    unnamed x258 -> x273, local copies, waits for them, and re-layouts: 22.8 us -> 23.6 us
where the time goes in v1:
time: 1110 us
  waiting for transfers between devices  376 us (34%)
  blocking collectives  294 us (26%)
  matrix products  176 us (16%)
  other arithmetic  145 us (13%)
  local copies, waits for them, and re-layouts  71.9 us (6%)
  starting transfers between devices  26.4 us (2%)
  between operations  16.6 us (1%)
    reduce_scatter x1, waiting for transfers between devices, body(): lax.psum_scatter(dot_f32(scaled, wo).astype(BF16), everyone, scatter_dime...  107 us
    reduce_scatter x1, waiting for transfers between devices, body(): lax.psum_scatter(part_normed.astype(BF16), everyone, scatter_dimension=0,...  105 us
    another operation x2, other arithmetic, mixer(): cum = jnp.cumsum(dt * -jnp.exp(a_log), axis=2)  95.2 us
    all_gather x1, waiting for transfers between devices, body(): cot = lax.all_gather(my_cot, everyone, axis=0, tiled=True)  76.9 us
    all_gather x3, blocking collectives, body(): lax.all_gather(a, 'seq', axis=a.ndim - 1, tiled=True)  62.7 us
    psum x1, blocking collectives, body(): lax.psum(jnp.stack([jnp.sum(gated * gated, axis=-1), jnp.sum(gs * gated,...  48.8 us
    psum x1, blocking collectives, body(): lax.psum((grad_norm, d_cbw, d_cbb), ('dp', 'seq', 'head'))  43.8 us
    all_gather x1, blocking collectives, body(): lax.all_gather(w_dt_in, ('dp', 'seq'), axis=0, tiled=True)  42.9 us
  transfers between devices with their start and end apart: 21, of which 9 were waited for; matrix products, arithmetic and copies ran while one was open for 16% of the time, Pallas kernels for 0%

profile of v1, /device:TPU:14, one launch (start us, length us, event | category | flops | bytes accessed | tf_op | source)
XLA Modules:
  0.0 1105.5 jit_solution(6930239819836706075)
XLA Ops:
  12.0 27.5 %all_to_all.101 = bf16[128,8,256]{0,2,1:T(8,128)(2,1)S(1)} all-to-all(bf16[128,8,256]{0,2,1:T(8,128)(2,1)S(1)} %bitcast.588), channel_id=1, replica_groups=mesh['dp'=2,'seq'=8,'head'=2] {'seq'}, dimensions={1} | all-to-all | bytes 1048576 | tf_op jit(solution)/shard_map/all_to_all | solution.py:139
  42.5 30.4 %all_to_all.102 = bf16[8,256,128]{1,2,0:T(8,128)(2,1)} all-to-all(bf16[8,256,128]{1,2,0:T(8,128)(2,1)S(1)} %bitcast_dynamic-update-slice_fusion.6), channel_id=1, replica_groups=mesh['dp'=2,'seq'=8,'head'=2] {'seq'}, dimensions={0} | all-to-all | bytes 1048576 | tf_op jit(solution)/shard_map/all_to_all | solution.py:153
  74.9 7.4 all-to-all-start.1
  84.1 42.9 %all_gather.47 = bf16[2048,32]{0,1:T(8,128)(2,1)S(1)} all-gather(bf16[128,32]{0,1:T(8,128)(2,1)S(1)} %copy-done.97), channel_id=1, replica_groups=mesh['dp'=2,'seq'=8,'head'=2] {'dp','seq'}, dimensions={0}, use_global_device_ids=true | all-gather | bytes 139264 | tf_op jit(solution)/shard_map/all_gather | solution.py:148
  131.0 5.6 fusion.19
  137.2 47.9 %fusion.185 = f32[2,8,128,4]{3,1,2,0:T(8,128)S(1)} fusion(f32[2,8,128,4]{3,1,2,0:T(8,128)S(1)} %copy.553), kind=kOutput, calls=%fused_computation.371 | output fusion | flops 1040384 | bytes 65536 | tf_op jit(solution)/shard_map/jvp(jit(cumsum))/reduce_window_sum | solution.py:41
  185.9 6.0 convolution_convert_fusion.6
  193.7 6.0 convolution_convert_fusion.5
  200.1 11.3 %all-gather.21.cloned.1.call-done = bf16[256,2048]{0,1:T(8,128)(2,1)} async-done(((bf16[256,1024]{0,1:T(8,128)(2,1)}), bf16[256,2048]{0,1:T(8,128)(2,1)}) %all-gather.21.cloned.1.call-update) | async-done | bytes 1048592 | tf_op jit(solution)/shard_map/all_gather | solution.py:151
  211.4 76.9 %all-gather.19.cloned.1.call-done = bf16[2048,2048]{1,0:T(8,128)(2,1)} async-done(((bf16[128,2048]{1,0:T(8,128)(2,1)}), bf16[2048,2048]{1,0:T(8,128)(2,1)}) %all-gather.19.cloned.1.call-update) | async-done | bytes 8388624 | tf_op jit(solution)/shard_map/all_gather | solution.py:160
  288.3 7.3 fusion.189
  298.8 11.7 %all-gather.17.cloned.1.call-done = bf16[2048,256]{1,0:T(8,128)(2,1)} async-done(((bf16[1024,256]{1,0:T(8,128)(2,1)}), bf16[2048,256]{1,0:T(8,128)(2,1)}) %all-gather.17.cloned.1.call-update) | async-done | bytes 1048592 | tf_op jit(solution)/shard_map/all_gather | solution.py:138
  310.5 6.0 convolution_convert_fusion.4
  321.9 6.9 fusion.44
  328.7 5.1 reshape.598
  333.8 4.9 copy.551
  357.1 10.7 multiply_reduce_fusion.16
  373.6 48.8 %psum.77 = f32[2,2,1024]{2,1,0:T(2,128)S(1)} all-reduce(f32[2,2,1024]{2,1,0:T(2,128)S(1)} %pad_maximum_fusion), channel_id=1, replica_groups=mesh['dp'=2,'seq'=8,'head'=2] {'seq','head'}, use_global_device_ids=true, to_apply=%region_4.5 | all-reduce | flops 4096 | bytes 32768 | tf_op jit(solution)/shard_map/psum | solution.py:191
  423.7 5.9 multiply_reduce_fusion.13
  455.7 12.5 %fusion.12 = (f32[2,8,128,128]{3,2,1,0:T(8,128)}, f32[2,8,128,128,4]{3,2,4,1,0:T(8,128)}) fusion(f32[2,8,128,4]{2,3,1,0:T(4,128)S(1)} %copy-done.72, pred[2,8,128,128]{3,2,1,0:T(8,128)(4,1)S(1)} %copy-done.51, pred[8,128,128]{2,1,0:T(8,128)(4,1)S(1)} %copy-done.56, f32[2,8,128,128]{3,2,1,0:T(8,128)S(1)} %copy-done.41, ...), kind=kOutput, calls=%fused_computation.18 | convolution fusion | flops 824442880 | bytes 10944512 | tf_op jit(solution)/shard_map/transpose(jvp(sktuh,skuhp->skthp))/dot_general | solution.py:74
  479.2 9.8 multiply_reduce_fusion
  492.4 47.3 %fusion.186 = f32[2,8,128,4]{3,1,2,0:T(8,128)S(1)} fusion(f32[2,8,128,4]{3,1,2,0:T(8,128)S(1)} %copy.645), kind=kOutput, calls=%fused_computation.372 | output fusion | flops 1040384 | bytes 65536 | tf_op jit(solution)/shard_map/transpose(jvp(jit(cumsum)))/reduce_window_sum | solution.py:41
  540.3 4.8 copy.694
  545.0 5.9 reshape.599
  566.6 8.1 fusion.156
  578.0 8.4 fusion.190
  586.4 16.1 %add_convert_fusion = bf16[2048,2048]{1,0:T(8,128)(2,1)} fusion(f32[2048,2048]{1,0:T(8,128)} %fusion.156, f32[2048,2048]{1,0:T(8,128)} %fusion.190, bf16[2048,256]{1,0:T(8,128)(2,1)S(1)} %bitcast.578, bf16[2048,256]{1,0:T(8,128)(2,1)S(1)} %copy-done.36), kind=kOutput, calls=%fused_computation | convolution fusion | flops 2160066560 | bytes 44040192 | tf_op jit(solution)/shard_map/rc,kc->rk/dot_general | solution.py:215
  604.0 5.6 convolution_convert_fusion
  609.7 6.9 fusion.191
  616.9 6.9 convolution_convert_fusion.3
  623.9 7.0 convolution_convert_fusion.2
  630.9 6.9 convolution_convert_fusion.1
  640.8 105.4 %reduce-scatter.13.cloned.1.call-done = bf16[128,2048]{1,0:T(8,128)(2,1)} async-done(((bf16[2048,2048]{1,0:T(8,128)(2,1)}), bf16[128,2048]{1,0:T(8,128)(2,1)}) %reduce-scatter.13.cloned.1.call-update) | async-done | bytes 524304 | tf_op jit(solution)/shard_map/reduce_scatter | solution.py:221
  748.3 107.0 %reduce-scatter.11.cloned.1.call-done = bf16[128,2048]{1,0:T(8,128)(2,1)} async-done(((bf16[2048,2048]{1,0:T(8,128)(2,1)}), bf16[128,2048]{1,0:T(8,128)(2,1)}) %reduce-scatter.11.cloned.1.call-update) | async-done | bytes 524304 | tf_op jit(solution)/shard_map/reduce_scatter | solution.py:197
  857.9 19.1 %reduce-scatter.25.cloned.1.call-done = f32[1024,4]{1,0:T(8,128)} async-done(((f32[2048,4]{1,0:T(8,128)}), f32[1024,4]{1,0:T(8,128)}) %reduce-scatter.25.cloned.1.call-update) | async-done | bytes 16400
  878.2 10.1 all_to_all.103
  888.3 11.9 %reduce-scatter.17.cloned.1.call-done = bf16[1024,256]{1,0:T(8,128)(2,1)} async-done(((bf16[2048,256]{1,0:T(8,128)(2,1)}), bf16[1024,256]{1,0:T(8,128)(2,1)}) %reduce-scatter.17.cloned.1.call-update) | async-done | bytes 524304 | tf_op jit(solution)/shard_map/reduce_scatter | solution.py:230
  900.2 6.1 all-to-all-start.3
  906.8 16.5 %reduce-scatter.19.cloned.1.call-done = bf16[1024,256]{1,0:T(8,128)(2,1)} async-done(((bf16[2048,256]{1,0:T(8,128)(2,1)}), bf16[1024,256]{1,0:T(8,128)(2,1)}) %reduce-scatter.19.cloned.1.call-update) | async-done | bytes 524304 | tf_op jit(solution)/shard_map/reduce_scatter | solution.py:230
  923.3 6.1 all-to-all-start.4
  930.8 15.1 %reduce-scatter.21.cloned.1.call-done = bf16[256,1024]{1,0:T(8,128)(2,1)} async-done(((bf16[256,2048]{1,0:T(8,128)(2,1)}), bf16[256,1024]{1,0:T(8,128)(2,1)}) %reduce-scatter.21.cloned.1.call-update) | async-done | bytes 524304 | tf_op jit(solution)/shard_map/reduce_scatter | solution.py:252
  947.8 6.1 all-to-all-start.6
  954.0 5.0 all-reduce.54
  959.0 19.6 %all-gather = f32[8,1,256]{2,1,0:T(1,128)S(1)} all-gather(f32[1,1,256]{2,1,0:T(1,128)S(1)} %bitcast.647), channel_id=1, replica_groups=mesh['dp'=2,'seq'=8,'head'=2] {'seq'}, dimensions={0}, use_global_device_ids=true | all-gather | bytes 9216 | tf_op jit(solution)/shard_map/all_gather | solution.py:263
  978.6 15.3 %all-gather.1 = f32[8,1,256]{2,1,0:T(1,128)S(1)} all-gather(f32[1,1,256]{2,1,0:T(1,128)S(1)} %bitcast.646), channel_id=1, replica_groups=mesh['dp'=2,'seq'=8,'head'=2] {'seq'}, dimensions={0}, use_global_device_ids=true | all-gather | bytes 9216 | tf_op jit(solution)/shard_map/all_gather | solution.py:263
  993.8 27.9 %all_gather.54 = f32[4,2048]{1,0:T(4,128)S(1)} all-gather(f32[4,256]{1,0:T(4,128)S(1)} %get-tuple-element.164), channel_id=1, replica_groups=mesh['dp'=2,'seq'=8,'head'=2] {'seq'}, dimensions={1}, use_global_device_ids=true | all-gather | bytes 36864 | tf_op jit(solution)/shard_map/all_gather | solution.py:263
  1022.3 22.3 %all-reduce.53 = (f32[32]{0:T(128)}, f32[32]{0:T(128)}, f32[32]{0:T(128)}) all-reduce(f32[32]{0:T(128)S(1)} %dynamic-update-slice, f32[32]{0:T(128)S(1)} %dynamic-update-slice.1, f32[32]{0:T(128)S(1)} %dynamic-update-slice.2), channel_id=1, replica_groups=mesh['dp'=2,'seq'=8,'head'=2] {'seq'}, use_global_device_ids=true, to_apply=%add.49 | all-reduce | flops 96 | bytes 768
  1048.1 43.8 %all-reduce.52 = (f32[2048]{0:T(1024)}, f32[4,256]{1,0:T(4,128)}, f32[256]{0:T(256)}) all-reduce(f32[2048]{0:T(1024)S(1)} %get-tuple-element.135, f32[4,256]{1,0:T(4,128)S(1)} %pad_add_fusion.10, f32[256]{0:T(256)S(1)} %get-tuple-element.131), channel_id=1, replica_groups=mesh['dp'=2,'seq'=8,'head'=2] {'dp','seq','head'}, use_global_device_ids=true, to_apply=%region_33.34 | all-reduce | flops 3328 | bytes 26624 | tf_op jit(solution)/shard_map/psum | solution.py:264
  (437 shorter events, 136.6 us)
Async XLA Ops:
  7.2 123.8 %all-gather.11.cloned.1.call-start = ((), (), s32[]{:S(2)}) async-start(), calls=%async_computation.15 | async-start | bytes 8912896 | tf_op jit(solution)/shard_map/all_gather | solution.py:135
  11.7 174.3 %all-gather.13.cloned.1.call-start = ((), (), s32[]{:S(2)}) async-start(), calls=%async_computation.16 | async-start | bytes 1572864 | tf_op jit(solution)/shard_map/all_gather | solution.py:138
  40.6 153.1 %all-gather.15.cloned.1.call-start = ((), (), s32[]{:S(2)}) async-start(), calls=%async_computation.17 | async-start | bytes 1114112 | tf_op jit(solution)/shard_map/all_gather | solution.py:150
  41.3 170.1 %all-gather.21.cloned.1.call-start = ((), (), s32[]{:S(2)}) async-start(), calls=%async_computation.20 | async-start | bytes 1572864 | tf_op jit(solution)/shard_map/all_gather | solution.py:151
  72.9 54.1 %copy-start.112 = (f32[32]{0:T(128)S(1)}, f32[32]{0:T(128)}, u32[]{:S(2)}) copy-start(f32[32]{0:T(128)} %param.27) | copy-start | bytes 388
  72.9 54.1 %copy-start.113 = (f32[32]{0:T(128)S(1)}, f32[32]{0:T(128)}, u32[]{:S(2)}) copy-start(f32[32]{0:T(128)} %param.29) | copy-start | bytes 388
  72.9 56.4 %copy-start.108 = (s32[2,1]{0,1:T(1,128)S(1)}, s32[2,1]{0,1:T(1,128)}, u32[]{:S(2)}) copy-start(s32[2,1]{0,1:T(1,128)} %param.32) | copy-start | bytes 28
  72.9 56.5 %copy-start.104 = (f32[4,256]{1,0:T(4,128)S(1)}, f32[4,256]{1,0:T(4,128)}, u32[]{:S(2)}) copy-start(f32[4,256]{1,0:T(4,128)} %param.25) | copy-start | bytes 12292
  72.9 215.4 %all-gather.19.cloned.1.call-start = ((), (), s32[]{:S(2)}) async-start(), calls=%async_computation.19 | async-start | bytes 8912896 | tf_op jit(solution)/shard_map/all_gather | solution.py:160
  74.9 55.0 %all-to-all-start.1 = ((bf16[128,8,256]{0,2,1:T(8,128)(2,1)}), bf16[128,8,256]{0,2,1:T(8,128)(2,1)S(1)}, u32[]{:S(2)}, u32[]{:S(2)}) async-start(bf16[128,8,256]{0,2,1:T(8,128)(2,1)} %bitcast.42), calls=%async_computation.1 | async-start | bytes 1048576 | tf_op jit(solution)/shard_map/all_to_all | solution.py:139
  82.3 228.2 %all-gather.17.cloned.1.call-start = ((), (), s32[]{:S(2)}) async-start(), calls=%async_computation.18 | async-start | bytes 1572864 | tf_op jit(solution)/shard_map/all_gather | solution.py:138
  82.4 54.3 %copy-start.100 = (f32[4]{0:T(128)}, f32[4]{0:T(128)S(1)}, u32[]{:S(2)}) copy-start(f32[4]{0:T(128)S(1)} %fusion.174) | copy-start | bytes 52
  83.3 238.5 %copy-start.81 = (f32[1,256]{1,0:T(1,128)}, f32[1,256]{1,0:T(1,128)S(1)}, u32[]{:S(2)}) copy-start(f32[1,256]{1,0:T(1,128)S(1)} %get-tuple-element.238) | copy-start | bytes 3076
  83.3 238.5 %copy-start.83 = (f32[1,256]{1,0:T(1,128)}, f32[1,256]{1,0:T(1,128)S(1)}, u32[]{:S(2)}) copy-start(f32[1,256]{1,0:T(1,128)S(1)} %get-tuple-element.239) | copy-start | bytes 3076
  83.3 238.5 %copy-start.85 = (f32[1,256]{1,0:T(1,128)}, f32[1,256]{1,0:T(1,128)S(1)}, u32[]{:S(2)}) copy-start(f32[1,256]{1,0:T(1,128)S(1)} %get-tuple-element.240) | copy-start | bytes 3076
  83.3 238.5 %copy-start.87 = (f32[1,256]{1,0:T(1,128)}, f32[1,256]{1,0:T(1,128)S(1)}, u32[]{:S(2)}) copy-start(f32[1,256]{1,0:T(1,128)S(1)} %get-tuple-element.241) | copy-start | bytes 3076
  127.1 229.9 %copy-start.115 = (f32[4]{0:T(128)}, f32[4]{0:T(128)S(1)}, u32[]{:S(2)}) copy-start(f32[4]{0:T(128)S(1)} %dynamic_slice.33) | copy-start | bytes 52
  129.4 70.3 %copy-start.67 = (pred[2,8,128]{2,1,0:T(8,128)(4,1)}, pred[2,8,128]{2,1,0:T(8,128)(4,1)S(1)}, u32[]{:S(2)}) copy-start(pred[2,8,128]{2,1,0:T(8,128)(4,1)S(1)} %broadcast_compare_fusion.2) | copy-start | bytes 6148
  129.4 209.3 %copy-start.89 = (f32[1,256]{1,0:T(1,128)}, f32[1,256]{1,0:T(1,128)S(1)}, u32[]{:S(2)}) copy-start(f32[1,256]{1,0:T(1,128)S(1)} %get-tuple-element.247) | copy-start | bytes 3076
  129.4 209.3 %copy-start.91 = (f32[1,256]{1,0:T(1,128)}, f32[1,256]{1,0:T(1,128)S(1)}, u32[]{:S(2)}) copy-start(f32[1,256]{1,0:T(1,128)S(1)} %get-tuple-element.248) | copy-start | bytes 3076
  129.4 209.3 %copy-start.93 = (f32[1,256]{1,0:T(1,128)}, f32[1,256]{1,0:T(1,128)S(1)}, u32[]{:S(2)}) copy-start(f32[1,256]{1,0:T(1,128)S(1)} %get-tuple-element.249) | copy-start | bytes 3076
  129.4 209.3 %copy-start.95 = (f32[1,256]{1,0:T(1,128)}, f32[1,256]{1,0:T(1,128)S(1)}, u32[]{:S(2)}) copy-start(f32[1,256]{1,0:T(1,128)S(1)} %get-tuple-element.250) | copy-start | bytes 3076
  129.7 227.4 %copy-start.55 = (pred[8,128,128]{2,1,0:T(8,128)(4,1)}, pred[8,128,128]{2,1,0:T(8,128)(4,1)S(1)}, u32[]{:S(2)}) copy-start(pred[8,128,128]{2,1,0:T(8,128)(4,1)S(1)} %get-tuple-element.245) | copy-start | bytes 393220
  129.8 227.2 %copy-start.50 = (pred[2,8,128,128]{3,2,1,0:T(8,128)(4,1)}, pred[2,8,128,128]{3,2,1,0:T(8,128)(4,1)S(1)}, u32[]{:S(2)}) copy-start(pred[2,8,128,128]{3,2,1,0:T(8,128)(4,1)S(1)} %broadcast_and_fusion) | copy-start | bytes 786436
  130.9 507.0 %reduce-scatter.15.cloned.1.call-start = ((), (), s32[]{:S(2)}) async-start(), calls=%async_computation.24 | async-start | bytes 2228224 | tf_op jit(solution)/shard_map/reduce_scatter | solution.py:210
  185.9 171.2 %copy-start.71 = (f32[2,8,128,4]{2,3,1,0:T(4,128)}, f32[2,8,128,4]{2,3,1,0:T(4,128)S(1)}, u32[]{:S(2)}) copy-start(f32[2,8,128,4]{2,3,1,0:T(4,128)S(1)} %copy.554) | copy-start | bytes 98308
  199.8 147.2 %copy-start.59 = (f32[2,8,128,4]{2,3,1,0:T(4,128)}, f32[2,8,128,4]{2,3,1,0:T(4,128)S(1)}, u32[]{:S(2)}) copy-start(f32[2,8,128,4]{2,3,1,0:T(4,128)S(1)} %copy.575) | copy-start | bytes 98308
  200.1 138.7 %copy-start = (f32[8,2,128,256]{3,2,0,1:T(8,128)}, f32[8,2,128,256]{3,2,0,1:T(8,128)S(1)}, u32[]{:S(2)}) copy-start(f32[8,2,128,256]{3,2,0,1:T(8,128)S(1)} %copy.552) | copy-start | bytes 6291460
  566.6 179.7 %reduce-scatter.13.cloned.1.call-start = ((), (), s32[]{:S(2)}) async-start(), calls=%async_computation.23 | async-start | bytes 8912896 | tf_op jit(solution)/shard_map/reduce_scatter | solution.py:221
  602.5 252.8 %reduce-scatter.11.cloned.1.call-start = ((), (), s32[]{:S(2)}) async-start(), calls=%async_computation.21 | async-start | bytes 8912896 | tf_op jit(solution)/shard_map/reduce_scatter | solution.py:197
  609.6 267.4 %reduce-scatter.25.cloned.1.call-start = ((), (), s32[]{:S(2)}) async-start(), calls=%async_computation.31 | async-start | bytes 1572864
  616.6 283.6 %reduce-scatter.17.cloned.1.call-start = ((), (), s32[]{:S(2)}) async-start(), calls=%async_computation.26 | async-start | bytes 1572864 | tf_op jit(solution)/shard_map/reduce_scatter | solution.py:230
  623.8 299.5 %reduce-scatter.19.cloned.1.call-start = ((), (), s32[]{:S(2)}) async-start(), calls=%async_computation.27 | async-start | bytes 1572864 | tf_op jit(solution)/shard_map/reduce_scatter | solution.py:230
  630.9 315.0 %reduce-scatter.21.cloned.1.call-start = ((), (), s32[]{:S(2)}) async-start(), calls=%async_computation.28 | async-start | bytes 1572864 | tf_op jit(solution)/shard_map/reduce_scatter | solution.py:252
  637.8 108.4 %copy-start.31 = (bf16[2,1,128,2048]{3,2,1,0:T(8,128)(2,1)S(1)}, bf16[2,1,128,2048]{3,2,1,0:T(8,128)(2,1)}, u32[]{:S(2)}) copy-start(bf16[2,1,128,2048]{3,2,1,0:T(8,128)(2,1)} %param.17) | copy-start | bytes 3145732
  637.8 108.4 %copy-start.62 = (f32[2048]{0:T(1024)S(1)}, f32[2048]{0:T(1024)}, u32[]{:S(2)}) copy-start(f32[2048]{0:T(1024)} %param.18) | copy-start | bytes 24580
  637.9 108.4 %copy-start.99 = (f32[128]{0:T(128)S(1)}, f32[128]{0:T(128)}, u32[]{:S(2)}) copy-start(f32[128]{0:T(128)} %copy-done.98) | copy-start | bytes 1540
  637.9 406.8 %reduce-scatter.23.cloned.1.call-start = ((), (), s32[]{:S(2)}) async-start(), calls=%async_computation.29 | async-start | bytes 2228224 | tf_op jit(solution)/shard_map/reduce_scatter | solution.py:245
  638.0 108.3 %copy-start.49 = (f32[128,256]{1,0:T(8,128)S(1)}, f32[128,256]{1,0:T(8,128)}, u32[]{:S(2)}) copy-start(f32[128,256]{1,0:T(8,128)} %reduce-scatter.15.cloned.1.call-done) | copy-start | bytes 393220
  640.7 107.5 %copy-start.111 = (f32[128]{0:T(128)S(1)}, f32[128]{0:T(128)}, u32[]{:S(2)}) copy-start(f32[128]{0:T(128)} %copy-done.110) | copy-start | bytes 1540
  640.8 214.5 %copy-start.44 = (bf16[2,1,128,2048]{3,2,1,0:T(8,128)(2,1)S(1)}, bf16[2,1,128,2048]{3,2,1,0:T(8,128)(2,1)}, u32[]{:S(2)}) copy-start(bf16[2,1,128,2048]{3,2,1,0:T(8,128)(2,1)} %param.33) | copy-start | bytes 3145732
  640.8 451.1 %all-gather.23.cloned.1.call-start = ((), (), s32[]{:S(2)}) async-start(), calls=%async_computation.22 | async-start | bytes 1572864 | tf_op jit(solution)/shard_map/all_gather | solution.py:260
  857.9 71.5 %copy-start.114 = (u32[32]{0:T(128)S(1)}, u32[32]{0:T(128)}, u32[]{:S(2)}) copy-start(u32[32]{0:T(128)} %constant.176) | copy-start | bytes 388
  900.2 23.1 %all-to-all-start.3 = ((bf16[8,128,256]{2,1,0:T(8,128)(2,1)}), bf16[8,128,256]{2,1,0:T(8,128)(2,1)S(1)}, u32[]{:S(2)}, u32[]{:S(2)}) async-start(bf16[8,128,256]{2,1,0:T(8,128)(2,1)} %bitcast.598), calls=%async_computation.7 | async-start | bytes 1048576 | tf_op jit(solution)/shard_map/all_to_all | solution.py:229
  906.2 185.7 %all-gather.25.cloned.1.call-start = ((), (), s32[]{:S(2)}) async-start(), calls=%async_computation.25 | async-start | bytes 3145728 | tf_op jit(solution)/shard_map/all_gather | solution.py:260
  923.3 24.5 %all-to-all-start.4 = ((bf16[8,128,256]{2,1,0:T(8,128)(2,1)}), bf16[8,128,256]{2,1,0:T(8,128)(2,1)S(1)}, u32[]{:S(2)}, u32[]{:S(2)}) async-start(bf16[8,128,256]{2,1,0:T(8,128)(2,1)} %bitcast.597), calls=%async_computation.9 | async-start | bytes 1048576 | tf_op jit(solution)/shard_map/all_to_all | solution.py:229
  947.8 99.2 %all-to-all-start.6 = ((bf16[256,8,128]{2,0,1:T(8,128)(2,1)}), bf16[256,8,128]{2,0,1:T(8,128)(2,1)S(1)}, u32[]{:S(2)}, u32[]{:S(2)}) async-start(bf16[256,8,128]{2,0,1:T(8,128)(2,1)} %copy_bitcast_fusion), calls=%async_computation.12 | async-start | bytes 1048576 | tf_op jit(solution)/shard_map/all_to_all | solution.py:251
  953.9 138.0 %all-reduce.57.cloned.1.call-start = ((), (), s32[]{:S(2)}) async-start(), calls=%async_computation.30 | async-start | bytes 262144 | tf_op jit(solution)/shard_map/psum | solution.py:246
  (90 other events, 875.1 us)
Sparse Core Ops, SparseCore 0:
  11.8 93.3 all-gather.10
  107.3 24.0 all-gather.12
  134.2 54.7 all-gather.14
  190.5 20.8 all-gather.20
  214.0 74.2 all-gather.18
  290.3 20.1 all-gather.16
  566.6 70.9 reduce-scatter.14
  642.2 103.9 reduce-scatter.12
  750.8 104.4 reduce-scatter.10
  858.0 18.9 reduce-scatter.24
  879.8 20.3 reduce-scatter.16
  902.9 20.3 reduce-scatter.18
  925.5 20.3 reduce-scatter.20
  948.7 76.7 reduce-scatter.22
  1026.9 14.2 all-gather.22
  1043.2 11.7 all-gather.24
  1057.3 19.0 all-reduce.56
